TPU v7x, 32 devices: a whole 2x2x4 slice. The times are simulated.
32 devices in a mesh: rows: 8 (over z, x), heads: 4 (over y, core).
Axes of the slice: x: 2, y: 2, z: 4, core: 2. Of those that a mesh axis runs over, the one named last changes fastest.
Arguments:
- patches: float32 [16384, 48], P(('rows', 'heads')), may hold values from -6 to 6
- segments: int32 [16384], P('rows'), may hold values from 0 to 3, as said below
- labels: int32 [64, 4], P(('rows', 'heads')), may hold values from 0 to 999
- w_in: bfloat16 [48, 768], replicated, may hold values from -0.875 to 0.875
- b_in: float32 [768], replicated, may hold values from -3 to 3
- pos_table: bfloat16 [256, 768], replicated, may hold values from -3 to 3
- cls_table: bfloat16 [1000, 768], replicated, may hold values from -3 to 3
- ln1_gain: float32 [1, 768], replicated, may hold values from 0.1 to 1.9
- ln1_bias: float32 [1, 768], replicated, may hold values from -2 to 2
- w_query: bfloat16 [1, 768, 768], P(None, None, 'heads'), may hold values from -0.21875 to 0.21875
- w_key: bfloat16 [1, 768, 768], P(None, None, 'heads'), may hold values from -0.21875 to 0.21875
- w_value: bfloat16 [1, 768, 768], P(None, None, 'heads'), may hold values from -0.21875 to 0.21875
- w_attn_out: bfloat16 [1, 768, 768], P(None, 'heads'), may hold values from -1.25 to 1.25
- ln2_gain: float32 [1, 768], replicated, may hold values from 0.1 to 1.9
- ln2_bias: float32 [1, 768], replicated, may hold values from -2 to 2
- w_up: bfloat16 [1, 768, 3072], P(None, None, 'heads'), may hold values from -0.21875 to 0.21875
- b_up: bfloat16 [1, 3072], P(None, 'heads'), may hold values from -3 to 3
- w_down: bfloat16 [1, 3072, 768], P(None, 'heads'), may hold values from -0.109375 to 0.109375
- b_down: float32 [1, 768], replicated, may hold values from -3 to 3
- w_out: bfloat16 [768, 96], replicated, may hold values from -0.02734375 to 0.02734375
- b_out: float32 [96], replicated, may hold values from -2 to 2
- latent_grad: float32 [16384, 48], P(('rows', 'heads')), may hold values from -6 to 6
- logdet_grad: float32 [16384], P(('rows', 'heads')), may hold values from -6 to 6
Outputs:
- latents: float32 [16384, 48], P(('rows', 'heads'))
- logdet: float32 [16384], P(('rows', 'heads'))
- patches_grad: float32 [16384, 48], P(('rows', 'heads'))
- scale_mean: float32 [64], P(('rows', 'heads'))
- scale_max: float32 [64], P(('rows', 'heads'))
- w_in_grad: float32 [48, 768], replicated
- b_in_grad: float32 [768], replicated
- pos_table_grad: float32 [256, 768], replicated
- cls_table_grad: float32 [1000, 768], replicated
- ln1_gain_grad: float32 [1, 768], replicated
- ln1_bias_grad: float32 [1, 768], replicated
- w_query_grad: float32 [1, 768, 768], P(None, None, 'heads')
- w_key_grad: float32 [1, 768, 768], P(None, None, 'heads')
- w_value_grad: float32 [1, 768, 768], P(None, None, 'heads')
- w_attn_out_grad: float32 [1, 768, 768], P(None, 'heads')
- ln2_gain_grad: float32 [1, 768], replicated
- ln2_bias_grad: float32 [1, 768], replicated
- w_up_grad: float32 [1, 768, 3072], P(None, None, 'heads')
- b_up_grad: float32 [1, 3072], P(None, 'heads')
- w_down_grad: float32 [1, 3072, 768], P(None, 'heads')
- b_down_grad: float32 [1, 768], replicated
- w_out_grad: float32 [768, 96], replicated
- b_out_grad: float32 [96], replicated
Inputs may be any that keep to these rules, and one draw needn't show every extreme that they name: Each row of 256 patches is either one segment numbered 0, or 4 segments of 64 patches numbered 0 to 3 in order; the first row is of the second kind.
All inputs are finite; a program needn't handle non-finite values.
Results may differ from a plain program's by a relative error of at most 0.034.
Values may be sent and summed in bfloat16 or wider, within the bound.
No kernel may reach another device: no remote copies, remote signals or barrier semaphores. Data moves between devices by JAX's collectives and lax.ppermute only.
A program may use at most 128 MiB of HBM per device.

v0:
```python
import jax
import jax.numpy as jnp
from jax import lax
from jax.sharding import PartitionSpec as P

HEAD_DIM = 64
EPSILON = 1e-05
PRECISE = lax.Precision.HIGHEST


def norm_rows(values, gains, offset):
    average = jnp.mean(values, -1, keepdims=True)
    centered = values - average
    spread = jnp.mean(centered * centered, -1, keepdims=True)
    return centered * lax.rsqrt(spread + EPSILON) * gains + offset


def gelu_exact(values):
    return jax.nn.gelu(values, approximate=False)


def matmul(matrix, other):
    return jnp.dot(matrix, other, preferred_element_type=jnp.float32)


def matmul_tn(matrix, other):
    return lax.dot_general(
        matrix, other, (((0,), (0,)), ((), ())), preferred_element_type=jnp.float32
    )


def matmul_nt(matrix, other):
    return lax.dot_general(
        matrix, other, (((1,), (1,)), ((), ())), preferred_element_type=jnp.float32
    )


def masked_scores(queries, key_rows, seg_block):
    length = seg_block.shape[-1]
    causal = lax.broadcasted_iota(jnp.int32, (length, length), 0) >= lax.broadcasted_iota(
        jnp.int32, (length, length), 1
    )
    allowed = (seg_block[:, :, None] == seg_block[:, None, :]) & causal[None]
    scores = jnp.einsum("bqhe,bkhe->bhqk", queries, key_rows, preferred_element_type=jnp.float32)
    return jnp.where(allowed[:, None], scores * HEAD_DIM ** (-0.5), -1e30)


def attend_forward(pieces):
    queries, key_rows, values, seg_block = pieces
    scores = masked_scores(queries, key_rows, seg_block)
    row_top = jnp.max(scores, -1, keepdims=True)
    denominator = jnp.sum(jnp.exp(scores - row_top), -1, keepdims=True)
    log_total = row_top + jnp.log(denominator)
    probs = jnp.exp(scores - log_total).astype(jnp.bfloat16)
    result = jnp.einsum("bhqk,bkhe->bqhe", probs, values, preferred_element_type=jnp.float32)
    return (result.astype(jnp.bfloat16), log_total)


def attend_backward(pieces):
    queries, key_rows, values, seg_block, log_total, grad_result = pieces
    scores = masked_scores(queries, key_rows, seg_block)
    probs = jnp.exp(scores - log_total)
    grad_probs = jnp.einsum(
        "bqhe,bkhe->bhqk", grad_result, values, preferred_element_type=jnp.float32
    )
    inner_sum = jnp.sum(probs * grad_probs, -1, keepdims=True)
    grad_scores = (probs * (grad_probs - inner_sum) * HEAD_DIM ** (-0.5)).astype(jnp.bfloat16)
    grad_query = jnp.einsum(
        "bhqk,bkhe->bqhe", grad_scores, key_rows, preferred_element_type=jnp.float32
    )
    grad_key = jnp.einsum(
        "bhqk,bqhe->bkhe", grad_scores, queries, preferred_element_type=jnp.float32
    )
    grad_value = jnp.einsum(
        "bhqk,bqhe->bkhe",
        probs.astype(jnp.bfloat16),
        grad_result,
        preferred_element_type=jnp.float32,
    )
    return (
        grad_query.astype(jnp.bfloat16),
        grad_key.astype(jnp.bfloat16),
        grad_value.astype(jnp.bfloat16),
    )


def per_device(
    patches,
    segments,
    labels,
    w_in,
    b_in,
    pos_table,
    cls_table,
    ln1_gain,
    ln1_bias,
    w_query,
    w_key,
    w_value,
    w_attn_out,
    ln2_gain,
    ln2_bias,
    w_up,
    b_up,
    w_down,
    b_down,
    w_out,
    b_out,
    latent_grad,
    logdet_grad,
):
    tokens_here = patches.shape[0]
    length = pos_table.shape[0]
    slot_count = labels.shape[1]
    channels = patches.shape[1]
    classes = cls_table.shape[0]
    width = pos_table.shape[1]
    heads_here = w_query.shape[2] // HEAD_DIM
    layers = w_query.shape[0]
    own_start = lax.axis_index("heads") * tokens_here
    own_segs = lax.dynamic_slice_in_dim(segments, own_start, tokens_here)
    seg_rows = own_segs.reshape(-1, length)
    row_count = seg_rows.shape[0]
    causal = lax.broadcasted_iota(jnp.int32, (length, length), 0) >= lax.broadcasted_iota(
        jnp.int32, (length, length), 1
    )
    matching = (seg_rows[:, :, None] == seg_rows[:, None, :]) & causal[None]
    position = (jnp.sum(matching.astype(jnp.int32), -1) - 1).reshape(-1)
    slot_ids = lax.broadcasted_iota(jnp.int32, (1, 1, slot_count), 2)
    token_label = jnp.sum(
        jnp.where(seg_rows[:, :, None] == slot_ids, labels[:, None, :], 0), -1
    ).reshape(-1)
    pos_onehot = (position[:, None] == lax.broadcasted_iota(jnp.int32, (1, length), 1)).astype(
        jnp.bfloat16
    )
    cls_onehot = (token_label[:, None] == lax.broadcasted_iota(jnp.int32, (1, classes), 1)).astype(
        jnp.bfloat16
    )
    patch_low = patches.astype(jnp.bfloat16)
    hidden = (
        matmul(patch_low, w_in)
        + b_in
        + matmul(pos_onehot, pos_table)
        + matmul(cls_onehot, cls_table)
    )
    group_rows = segments.shape[0] // length
    blocks = group_rows // 2
    seg_blocks = segments.reshape(blocks, 2, length)

    def to_blocks(matrix):
        return matrix.reshape(blocks, 2, length, heads_here, HEAD_DIM)

    def from_blocks(tensor):
        return tensor.reshape(group_rows * length, heads_here * HEAD_DIM)

    depth = 0
    normed1 = norm_rows(hidden, ln1_gain[depth], ln1_bias[depth]).astype(jnp.bfloat16)
    rows_norm = lax.all_gather(normed1, "heads", axis=0, tiled=True)
    queries = matmul(rows_norm, w_query[depth]).astype(jnp.bfloat16)
    key_rows = matmul(rows_norm, w_key[depth]).astype(jnp.bfloat16)
    values = matmul(rows_norm, w_value[depth]).astype(jnp.bfloat16)
    attended, log_total = lax.map(
        attend_forward, (to_blocks(queries), to_blocks(key_rows), to_blocks(values), seg_blocks)
    )
    attended = from_blocks(attended)
    weight_out = w_attn_out[depth]
    attn_mix = lax.psum_scatter(
        matmul(attended, weight_out).astype(jnp.bfloat16), "heads", scatter_dimension=0, tiled=True
    ).astype(jnp.float32)
    hidden1 = hidden + attn_mix
    normed2 = norm_rows(hidden1, ln2_gain[depth], ln2_bias[depth]).astype(jnp.bfloat16)
    mlp_input = lax.all_gather(normed2, "heads", axis=0, tiled=True)
    full_up = w_up[depth]
    full_bias = b_up[depth]
    full_down = w_down[depth]
    pre_act = matmul(mlp_input, full_up) + full_bias.astype(jnp.float32)
    activated = gelu_exact(pre_act).astype(jnp.bfloat16)
    branch = lax.psum_scatter(
        matmul(activated, full_down).astype(jnp.bfloat16), "heads", scatter_dimension=0, tiled=True
    ).astype(jnp.float32)
    hidden2 = hidden1 + branch + b_down[depth]
    stored = [
        (
            hidden,
            rows_norm,
            queries,
            key_rows,
            values,
            attended,
            log_total,
            hidden1,
            mlp_input,
            pre_act,
            activated,
            full_up,
            full_down,
        )
    ]
    top_low = hidden2.astype(jnp.bfloat16)
    head_out = matmul(top_low, w_out) + b_out
    carried = jnp.concatenate(
        [jnp.zeros((row_count, 1), dtype=bool), seg_rows[:, 1:] == seg_rows[:, :-1]], 1
    ).reshape(-1)

    def flow_head(head_vals, patch_vals):
        previous = jnp.concatenate([jnp.zeros_like(head_vals[:1]), head_vals[:-1]], 0)
        previous = jnp.where(carried[:, None], previous, 0.0)
        shifts = previous[:, :channels]
        logscale = previous[:, channels:]
        latent_vals = (patch_vals - shifts) * jnp.exp(-logscale)
        return ((latent_vals, -jnp.sum(logscale, -1)), logscale)

    (latents, logdet), head_pull, logscale = jax.vjp(flow_head, head_out, patches, has_aux=True)
    grad_head, grad_direct = head_pull((latent_grad, logdet_grad))
    scale_rows = logscale.reshape(row_count, -1)
    scale_mean = jnp.mean(scale_rows, -1)
    scale_max = jnp.max(scale_rows, -1)
    grad_low = grad_head.astype(jnp.bfloat16)
    grad_w_out = matmul_tn(top_low, grad_low)
    grad_b_out = jnp.sum(grad_low.astype(jnp.float32), 0)
    grad_hidden = matmul_nt(grad_low, w_out)
    per_layer = [None] * layers
    for depth in reversed(range(layers)):
        (
            hidden0,
            rows_norm,
            queries,
            key_rows,
            values,
            attended,
            log_total,
            hidden1,
            mlp_input,
            pre_act,
            activated,
            full_up,
            full_down,
        ) = stored[depth]
        grad_b_down = jnp.sum(grad_hidden, 0)
        grad_branch = grad_hidden.astype(jnp.bfloat16)
        grad_branch_rows = lax.all_gather(grad_branch, "heads", axis=0, tiled=True)
        grad_activated = matmul_nt(grad_branch_rows, full_down)
        gelu_values, gelu_pull = jax.vjp(gelu_exact, pre_act)
        grad_pre = gelu_pull(grad_activated)[0].astype(jnp.bfloat16)
        grad_w_down = matmul_tn(activated, grad_branch_rows)
        grad_w_up = matmul_tn(mlp_input, grad_pre)
        grad_b_up = jnp.sum(grad_pre.astype(jnp.float32), 0)
        grad_normed2 = lax.psum_scatter(
            matmul_nt(grad_pre, full_up).astype(jnp.bfloat16),
            "heads",
            scatter_dimension=0,
            tiled=True,
        ).astype(jnp.float32)
        norm_values, norm_pull = jax.vjp(norm_rows, hidden1, ln2_gain[depth], ln2_bias[depth])
        back_hidden1, grad_gain2, grad_bias2 = norm_pull(grad_normed2)
        grad_hidden1 = grad_hidden + back_hidden1
        grad_mix = grad_hidden1.astype(jnp.bfloat16)
        grad_mix_rows = lax.all_gather(grad_mix, "heads", axis=0, tiled=True)
        weight_out = w_attn_out[depth]
        grad_attended = matmul_nt(grad_mix_rows, weight_out).astype(jnp.bfloat16)
        grad_w_attn = matmul_tn(attended, grad_mix_rows)
        grad_query, grad_key, grad_value = lax.map(
            attend_backward,
            (
                to_blocks(queries),
                to_blocks(key_rows),
                to_blocks(values),
                seg_blocks,
                log_total,
                to_blocks(grad_attended),
            ),
        )
        grad_query = from_blocks(grad_query)
        grad_key = from_blocks(grad_key)
        grad_value = from_blocks(grad_value)
        grad_w_query = matmul_tn(rows_norm, grad_query)
        grad_w_key = matmul_tn(rows_norm, grad_key)
        grad_w_value = matmul_tn(rows_norm, grad_value)
        weight_query, weight_key, weight_value = (w_query[depth], w_key[depth], w_value[depth])
        total = matmul_nt(grad_query, weight_query)
        total = total + matmul_nt(grad_key, weight_key)
        grad_normed1 = lax.psum_scatter(
            (total + matmul_nt(grad_value, weight_value)).astype(jnp.bfloat16),
            "heads",
            scatter_dimension=0,
            tiled=True,
        ).astype(jnp.float32)
        norm_values1, norm_pull1 = jax.vjp(norm_rows, hidden0, ln1_gain[depth], ln1_bias[depth])
        back_hidden0, grad_gain1, grad_bias1 = norm_pull1(grad_normed1)
        grad_hidden = grad_hidden1 + back_hidden0
        per_layer[depth] = (
            grad_w_query,
            grad_w_key,
            grad_w_value,
            grad_w_attn,
            grad_w_up,
            grad_b_up,
            grad_w_down,
            grad_gain1,
            grad_bias1,
            grad_gain2,
            grad_bias2,
            grad_b_down,
        )

    def stacked(index):
        return jnp.stack([entry[index] for entry in per_layer], 0)

    grad_embed = grad_hidden.astype(jnp.bfloat16)
    grad_w_in = matmul_tn(patch_low, grad_embed)
    grad_b_in = jnp.sum(grad_embed.astype(jnp.float32), 0)
    patches_grad = grad_direct + matmul_nt(grad_embed, w_in)
    quarter = length // slot_count
    packed_row = seg_rows[:, -1] > 0
    grad_slots = grad_hidden.reshape(row_count, slot_count, quarter, width)
    single_part = jnp.sum(
        jnp.where(packed_row[:, None, None], 0.0, grad_hidden.reshape(row_count, length, width)), 0
    )
    packed_part = jnp.sum(jnp.where(packed_row[:, None, None, None], grad_slots, 0.0), (0, 1))
    grad_pos = single_part + jnp.concatenate(
        [packed_part, jnp.zeros((length - quarter, width), jnp.float32)], 0
    )
    slot_sums = jnp.sum(grad_slots, 2)
    row_total = jnp.sum(slot_sums, 1)
    first_slot = lax.broadcasted_iota(jnp.int32, (1, slot_count, 1), 1) == 0
    slot_vectors = jnp.where(
        packed_row[:, None, None], slot_sums, jnp.where(first_slot, row_total[:, None, :], 0.0)
    )
    label_onehot = (
        labels.reshape(-1)[:, None] == lax.broadcasted_iota(jnp.int32, (1, classes), 1)
    ).astype(jnp.float32)
    grad_cls = lax.dot_general(
        label_onehot, slot_vectors.reshape(-1, width), (((0,), (0,)), ((), ())), precision=PRECISE
    )
    sum_query, sum_key, sum_value, sum_attn, sum_up, sum_b_up, sum_down = lax.psum(
        (stacked(0), stacked(1), stacked(2), stacked(3), stacked(4), stacked(5), stacked(6)), "rows"
    )
    (
        sum_w_in,
        sum_b_in,
        sum_pos,
        sum_cls,
        sum_gain1,
        sum_bias1,
        sum_gain2,
        sum_bias2,
        sum_b_down,
        sum_w_out,
        sum_b_out,
    ) = lax.psum(
        (
            grad_w_in,
            grad_b_in,
            grad_pos,
            grad_cls,
            stacked(7),
            stacked(8),
            stacked(9),
            stacked(10),
            stacked(11),
            grad_w_out,
            grad_b_out,
        ),
        ("rows", "heads"),
    )
    return (
        latents,
        logdet,
        patches_grad,
        scale_mean,
        scale_max,
        sum_w_in,
        sum_b_in,
        sum_pos,
        sum_cls,
        sum_gain1,
        sum_bias1,
        sum_query,
        sum_key,
        sum_value,
        sum_attn,
        sum_gain2,
        sum_bias2,
        sum_up,
        sum_b_up,
        sum_down,
        sum_b_down,
        sum_w_out,
        sum_b_out,
    )


def solution(mesh):
    in_specs = (
        P(("rows", "heads"), None),
        P("rows"),
        P(("rows", "heads"), None),
        P(),
        P(),
        P(),
        P(),
        P(),
        P(),
        P(None, None, "heads"),
        P(None, None, "heads"),
        P(None, None, "heads"),
        P(None, "heads", None),
        P(),
        P(),
        P(None, None, "heads"),
        P(None, "heads"),
        P(None, "heads", None),
        P(),
        P(),
        P(),
        P(("rows", "heads"), None),
        P(("rows", "heads")),
    )
    out_specs = (
        P(("rows", "heads"), None),
        P(("rows", "heads")),
        P(("rows", "heads"), None),
        P(("rows", "heads")),
        P(("rows", "heads")),
        P(),
        P(),
        P(),
        P(),
        P(),
        P(),
        P(None, None, "heads"),
        P(None, None, "heads"),
        P(None, None, "heads"),
        P(None, "heads", None),
        P(),
        P(),
        P(None, None, "heads"),
        P(None, "heads"),
        P(None, "heads", None),
        P(),
        P(),
        P(),
    )
    return jax.shard_map(
        per_device, mesh=mesh, in_specs=in_specs, out_specs=out_specs, check_vma=False
    )
```

profile of v0, /device:TPU:0, one launch (start us, length us, event | category | flops | bytes accessed | tf_op | source)
XLA Modules:
  0.0 903.8 jit_solution(2534567188782438305)
XLA Ops:
  14.6 31.1 %all-gather.5.cloned.1.call-done = bf16[2048,768]{1,0:T(8,128)(2,1)} async-done(((bf16[512,768]{1,0:T(8,128)(2,1)}), bf16[2048,768]{1,0:T(8,128)(2,1)}) %all-gather.5.cloned.1.call-update) | async-done | bytes 3145744 | tf_op jit(solution)/shard_map/all_gather | solution.py:158
  51.6 3.9 convolution_convert_fusion.7
  61.0 3.9 convolution_convert_fusion.6
  71.7 12.9 %while.26 = (s32[]{:T(128)}, bf16[4,2,256,3,64]{2,1,0,4,3:T(2,128)(2,1)}, f32[4,2,3,256,1]{3,2,1,4,0:T(4,128)S(1)}, bf16[4,2,256,3,64]{2,4,3,1,0:T(8,128)(2,1)S(...) while((s32[]{:T(128)}, ...), condition=%wide.region_7.8_spmd, body=%wide.region_4.7_spmd.sunk | while | flops 103840256 | bytes 6358625 | solution.py:162
  91.4 37.4 %reduce-scatter.5.cloned.1.call-done = bf16[512,768]{1,0:T(8,128)(2,1)} async-done(((bf16[2048,768]{1,0:T(8,128)(2,1)}), bf16[512,768]{1,0:T(8,128)(2,1)}) %reduce-scatter.5.cloned.1.call-update) | async-done | bytes 786448 | tf_op jit(solution)/shard_map/reduce_scatter | solution.py:167
  132.9 28.4 %all-gather.7.cloned.1.call-done = bf16[2048,768]{1,0:T(8,128)(2,1)} async-done(((bf16[512,768]{1,0:T(8,128)(2,1)}), bf16[2048,768]{1,0:T(8,128)(2,1)}) %all-gather.7.cloned.1.call-update) | async-done | bytes 3145744 | tf_op jit(solution)/shard_map/all_gather | solution.py:172
  161.3 18.8 %multiply_convert_fusion.1 = (bf16[2048,768]{1,0:T(8,128)(2,1)S(1)}, f32[2048,768]{1,0:T(8,128)}, f32[2048,768]{1,0:T(8,128)}) fusion(f32[768]{0:T(1024)S(1)} %convert_reduce_fusion.6, bf16[2048,768]{1,0:T(8,128)(2,1)} %all-gather.7.cloned.1.call-done, bf16[1,768,768]{2,1,0:T(8,128)(2,1)} %param.42), kind=kOutput, calls=%fused_computation.70 | convolution fusion | flops 2519728128 | bytes 20057088 | tf_op jit(solution)/shard_map/dot_general | solution.py:23
  181.8 3.9 convolution_convert_fusion.3
  186.7 37.1 %reduce-scatter.7.cloned.1.call-done = bf16[512,768]{1,0:T(8,128)(2,1)} async-done(((bf16[2048,768]{1,0:T(8,128)(2,1)}), bf16[512,768]{1,0:T(8,128)(2,1)}) %reduce-scatter.7.cloned.1.call-update) | async-done | bytes 786448 | tf_op jit(solution)/shard_map/reduce_scatter | solution.py:178
  229.8 28.6 %all-gather.9.cloned.1.call-done = bf16[2048,768]{1,0:T(8,128)(2,1)} async-done(((bf16[512,768]{1,0:T(8,128)(2,1)}), bf16[2048,768]{1,0:T(8,128)(2,1)}) %all-gather.9.cloned.1.call-update) | async-done | bytes 3145744 | tf_op jit(solution)/shard_map/all_gather | solution.py:241
  258.5 11.2 %convert_reduce_fusion = (f32[768]{0:T(1024)}, bf16[2048,768]{1,0:T(8,128)(2,1)S(1)}) fusion(f32[2048,768]{1,0:T(8,128)} %get-tuple-element.240, bf16[2048,768]{1,0:T(8,128)(2,1)} %all-gather.9.cloned.1.call-done, bf16[1,768,768]{2,1,0:T(8,128)(2,1)} %param.44, f32[2048,768]{1,0:T(8,128)} %get-tuple-element.255, f32[768]{0:T(1024)S(1)} %convert_reduce_fusion.6), kind=kOutput, calls=%fused_computation.67 | convolution fusion | flops 2442657024 | bytes 20060160 | tf_op jit(solution)/shard_map/dot_general | solution.py:33
  271.3 4.0 convolution_convert_fusion.2
  275.8 37.7 %reduce-scatter.9.cloned.1.call-done = bf16[512,768]{1,0:T(8,128)(2,1)} async-done(((bf16[2048,768]{1,0:T(8,128)(2,1)}), bf16[512,768]{1,0:T(8,128)(2,1)}) %reduce-scatter.9.cloned.1.call-update) | async-done | bytes 786448 | tf_op jit(solution)/shard_map/reduce_scatter | solution.py:248
  321.0 28.6 %all-gather.11.cloned.1.call-done = bf16[2048,768]{1,0:T(8,128)(2,1)} async-done(((bf16[512,768]{1,0:T(8,128)(2,1)}), bf16[2048,768]{1,0:T(8,128)(2,1)}) %all-gather.11.cloned.1.call-update) | async-done | bytes 3145744 | tf_op jit(solution)/shard_map/all_gather | solution.py:258
  349.7 3.9 convolution_convert_fusion.5
  360.8 69.2 %while.27 = (s32[]{:T(128)}, bf16[4,2,256,3,64]{2,1,0,4,3:T(2,128)(2,1)}, bf16[4,2,256,3,64]{2,1,0,4,3:T(2,128)(2,1)}, bf16[4,2,256,3,64]{2,1,0,4,3:T(2,128)(2,1...) while((s32[]{:T(128)}, ...), condition=%wide.region_18.19_spmd, body=%wide.region_16.18_spmd.sunk | while | flops 257789440 | bytes 21261944 | solution.py:262
  367.3 3.5 fusion.190
  373.8 3.5 fusion.188
  384.6 3.5 fusion.190
  391.1 3.5 fusion.188
  401.9 3.5 fusion.190
  408.4 3.4 fusion.188
  419.2 3.5 fusion.190
  425.7 3.4 fusion.188
  446.1 7.1 convolution_bitcast_fusion
  453.1 4.1 convolution_bitcast_fusion.1
  466.6 17.5 %reduce-scatter.11.cloned.1.call-done = bf16[512,768]{1,0:T(8,128)(2,1)} async-done(((bf16[2048,768]{1,0:T(8,128)(2,1)}), bf16[512,768]{1,0:T(8,128)(2,1)}) %reduce-scatter.11.cloned.1.call-update) | async-done | bytes 786448 | tf_op jit(solution)/shard_map/reduce_scatter | solution.py:282
  498.8 22.7 %psum.139 = f32[1,768]{1,0:T(1,128)} all-reduce(f32[1,768]{1,0:T(1,128)S(1)} %stack.33), channel_id=1, replica_groups=mesh['rows'=8,'heads'=4] {'rows'}, use_global_device_ids=true, to_apply=%region_48.49 | all-reduce | flops 768 | bytes 6144 | tf_op jit(solution)/shard_map/psum | solution.py:335
  521.5 41.5 %all-reduce.6 = (f32[768]{0:T(1024)}, f32[1,768]{1,0:T(1,128)}, f32[1,768]{1,0:T(1,128)}, f32[1,768]{1,0:T(1,128)}, f32[1,768]{1,0:T(1,128)}, /*index=5*/f32[1,768]{1,0:T(1,128)}, f32[96]{0:T(128)}) all-reduce(f32[768]{0:T(1024)S(1)} %get-tuple-element.235, ...), channel_id=1, replica_groups=mesh['rows'=8,'heads'=4] {'rows','heads'}, use_global_device_ids=true, to_apply=%region_27.28 | all-reduce | flops 4704 | bytes 37632 | tf_op jit(solution)/shard_map/psum | solution.py:350
  564.0 165.1 %all-reduce.14.cloned.1.call-done = (f32[1,768,192]{1,2,0:T(8,128)}, f32[1,768,192]{1,2,0:T(8,128)}, f32[1,768,192]{1,2,0:T(8,128)}, f32[1,192,768]{2,1,0:T(8,12...) async-done(((f32[1,768,192]{1,2,0:T(8,128)}, f32[1,768,192]{1,2,0:T(8,128)}, f32[1,768,192]{1,2,0:T(8,128)}, f32[1,192,768]{2,1,0:T(8,128)}, f32[1,768,768]{2,1,0:T(8,128)}, ...) | async-done | bytes 7077904 | tf_op jit(solution)/shard_map/psum | solution.py:335
  729.1 152.3 %all-reduce.12.cloned.1.call-done = (f32[48,768]{1,0:T(8,128)}, f32[256,768]{1,0:T(8,128)}, f32[1000,768]{1,0:T(8,128)}, f32[768,96]{0,1:T(8,128)}) async-done(((f32[48,768]{1,0:T(8,128)}, f32[256,768]{1,0:T(8,128)}, f32[1000,768]{1,0:T(8,128)}, f32[768,96]{0,1:T(8,128)}), (f32[48,768]{1,0:T(8,128)}, f32[256,768]{1,0:T(8,128)}, f32[1000,768]{1,0:T(8,128)}, ...) | async-done | bytes 4300816 | tf_op jit(solution)/shard_map/psum | solution.py:350
  885.0 3.8 copy.163
  (332 shorter events, 168.0 us)
Async XLA Ops:
  7.2 3.9 copy-start
  7.2 3.5 copy-start.23
  7.2 3.5 copy-start.36
  7.2 38.5 %all-gather.5.cloned.1.call-start = ((), (), s32[]{:S(2)}) async-start(), calls=%async_computation.4 | async-start | bytes 3932160 | tf_op jit(solution)/shard_map/all_gather | solution.py:158
  13.1 32.6 %copy-start.40 = (bf16[1,768,192]{1,2,0:T(8,128)(2,1)S(1)}, bf16[1,768,192]{1,2,0:T(8,128)(2,1)}, u32[]{:S(2)}) copy-start(bf16[1,768,192]{1,2,0:T(8,128)(2,1)} %param.38) | copy-start | bytes 884740
  14.3 114.5 %reduce-scatter.5.cloned.1.call-start = ((), (), s32[]{:S(2)}) async-start(), calls=%async_computation.5 | async-start | bytes 3932160 | tf_op jit(solution)/shard_map/reduce_scatter | solution.py:167
  55.5 5.5 copy-start.31
  90.7 70.6 %all-gather.7.cloned.1.call-start = ((), (), s32[]{:S(2)}) async-start(), calls=%async_computation.6 | async-start | bytes 3932160 | tf_op jit(solution)/shard_map/all_gather | solution.py:172
  132.6 91.2 %reduce-scatter.7.cloned.1.call-start = ((), (), s32[]{:S(2)}) async-start(), calls=%async_computation.7 | async-start | bytes 3932160 | tf_op jit(solution)/shard_map/reduce_scatter | solution.py:178
  161.3 20.5 %copy-start.57 = (bf16[1,768,768]{2,1,0:T(8,128)(2,1)S(1)}, bf16[1,768,768]{2,1,0:T(8,128)(2,1)}, u32[]{:S(2)}) copy-start(bf16[1,768,768]{2,1,0:T(8,128)(2,1)} %param.44) | copy-start | bytes 3538948
  185.7 72.8 %all-gather.9.cloned.1.call-start = ((), (), s32[]{:S(2)}) async-start(), calls=%async_computation.8 | async-start | bytes 3932160 | tf_op jit(solution)/shard_map/all_gather | solution.py:241
  186.7 38.9 %copy-start.24 = (bf16[768,96]{0,1:T(8,128)(2,1)S(1)}, bf16[768,96]{0,1:T(8,128)(2,1)}, u32[]{:S(2)}) copy-start(bf16[768,96]{0,1:T(8,128)(2,1)} %param.46) | copy-start | bytes 442372
  186.7 39.3 %copy-start.55 = (f32[96]{0:T(128)S(1)}, f32[96]{0:T(128)}, u32[]{:S(2)}) copy-start(f32[96]{0:T(128)} %param.47) | copy-start | bytes 1156
  225.6 4.2 copy-start.16
  229.8 83.7 %reduce-scatter.9.cloned.1.call-start = ((), (), s32[]{:S(2)}) async-start(), calls=%async_computation.9 | async-start | bytes 3932160 | tf_op jit(solution)/shard_map/reduce_scatter | solution.py:248
  258.5 12.8 %copy-start.58 = (bf16[1,768,768]{2,1,0:T(8,128)(2,1)S(1)}, bf16[1,768,768]{2,1,0:T(8,128)(2,1)}, u32[]{:S(2)}) copy-start(bf16[1,768,768]{2,1,0:T(8,128)(2,1)} %param.42) | copy-start | bytes 3538948
  275.4 74.3 %all-gather.11.cloned.1.call-start = ((), (), s32[]{:S(2)}) async-start(), calls=%async_computation.10 | async-start | bytes 3932160 | tf_op jit(solution)/shard_map/all_gather | solution.py:258
  319.9 29.8 %copy-start.39 = (bf16[1,192,768]{2,1,0:T(8,128)(2,1)S(1)}, bf16[1,192,768]{2,1,0:T(8,128)(2,1)}, u32[]{:S(2)}) copy-start(bf16[1,192,768]{2,1,0:T(8,128)(2,1)} %param.39) | copy-start | bytes 884740
  321.0 163.1 %reduce-scatter.11.cloned.1.call-start = ((), (), s32[]{:S(2)}) async-start(), calls=%async_computation.11 | async-start | bytes 3932160 | tf_op jit(solution)/shard_map/reduce_scatter | solution.py:282
  433.1 6.5 copy-start.32
  446.0 283.1 %all-reduce.14.cloned.1.call-start = ((), (), s32[]{:S(2)}) async-start(), calls=%async_computation.13 | async-start | bytes 14155776 | tf_op jit(solution)/shard_map/psum | solution.py:335
  446.0 7.1 copy-start.56
  446.0 7.1 copy-start.62
  453.1 4.1 copy-start.19
  464.5 416.9 %all-reduce.12.cloned.1.call-start = ((), (), s32[]{:S(2)}) async-start(), calls=%async_computation.12 | async-start | bytes 8601600 | tf_op jit(solution)/shard_map/psum | solution.py:350
  496.7 24.8 %copy-start.43 = (f32[768]{0:T(1024)S(1)}, f32[768]{0:T(1024)}, u32[]{:S(2)}) copy-start(f32[768]{0:T(1024)} %get-tuple-element.173) | copy-start | bytes 9220
  496.7 24.8 %copy-start.42 = (f32[768]{0:T(1024)S(1)}, f32[768]{0:T(1024)}, u32[]{:S(2)}) copy-start(f32[768]{0:T(1024)} %get-tuple-element.177) | copy-start | bytes 9220
  496.7 66.3 %copy-start.30 = (f32[512,48]{0,1:T(8,128)S(1)}, f32[512,48]{0,1:T(8,128)}, u32[]{:S(2)}) copy-start(f32[512,48]{0,1:T(8,128)} %param.48) | copy-start | bytes 294916
  496.7 66.3 %copy-start.37 = (bf16[48,768]{1,0:T(8,128)(2,1)S(1)}, bf16[48,768]{1,0:T(8,128)(2,1)}, u32[]{:S(2)}) copy-start(bf16[48,768]{1,0:T(8,128)(2,1)} %param.30) | copy-start | bytes 221188
  885.0 3.8 copy-start.28
  885.0 4.6 copy-start.27
  892.1 4.6 copy-start.1
  (41 other events, 67.2 us)
Sparse Core Ops, SparseCore 0:
  14.5 31.2 all-gather.4
  90.8 37.9 reduce-scatter.4
  132.7 28.5 all-gather.6
  185.8 37.9 reduce-scatter.6
  229.9 28.5 all-gather.8
  275.5 37.9 reduce-scatter.8
  321.1 28.5 all-gather.10
  446.1 37.9 reduce-scatter.10
  490.3 238.7 all-reduce.13
  737.9 143.3 all-reduce.11
where the time goes:
time: 908 us; the launch traced here: 904 us
  waiting for transfers between devices  564 us (62%)
  matrix products  154 us (17%)
  local copies, waits for them, and re-layouts  78.6 us (9%)
  blocking collectives  64.2 us (7%)
  other arithmetic  26.4 us (3%)
  between operations  15.1 us (2%)
    psum x1, waiting for transfers between devices, per_device(): lax.psum((stacked(0), stacked(1), stacked(2), stacked(3), stacked(4), sta...  165 us
    psum x1, waiting for transfers between devices, per_device(): lax.psum((grad_w_in, grad_b_in, grad_pos, grad_cls, stacked(7), stacked(8...  152 us
    psum x1, blocking collectives, per_device(): lax.psum((grad_w_in, grad_b_in, grad_pos, grad_cls, stacked(7), stacked(8...  41.5 us
    dot_general x10, matrix products, matmul(): return jnp.dot(matrix, other, preferred_element_type=jnp.float32)  39.8 us
    reduce_scatter x1, waiting for transfers between devices, per_device(): lax.psum_scatter(matmul_nt(grad_pre, full_up).astype(jnp.bfloat16), 'head...  37.7 us
    reduce_scatter x1, waiting for transfers between devices, per_device(): lax.psum_scatter(matmul(attended, weight_out).astype(jnp.bfloat16), 'head...  37.4 us
    reduce_scatter x1, waiting for transfers between devices, per_device(): lax.psum_scatter(matmul(activated, full_down).astype(jnp.bfloat16), 'head...  37.1 us
    all_gather x1, waiting for transfers between devices, per_device(): rows_norm = lax.all_gather(normed1, 'heads', axis=0, tiled=True)  31.1 us
  transfers between devices with their start and end apart: 10, of which 10 were waited for; matrix products, arithmetic and copies ran while one was open for 4% of the time, Pallas kernels for 0%

commit v1 on v0

--- a/solution.py
+++ b/solution.py
@@ -6,6 +6,27 @@
 HEAD_DIM = 64
 EPSILON = 1e-05
 PRECISE = lax.Precision.HIGHEST
+
+
+def ring_gather(value, axis, dim):
+    length, index, rows = (lax.axis_size(axis), lax.axis_index(axis), value.shape[dim])
+    right = [(i, (i + 1) % length) for i in range(length)]
+    left = [(i, (i - 1) % length) for i in range(length)]
+    out = jnp.zeros((*value.shape[:dim], length * rows, *value.shape[dim + 1 :]), value.dtype)
+    out = lax.dynamic_update_slice_in_dim(out, value, index * rows, axis=dim)
+    from_left = from_right = value
+    halfway = length // 2
+    for lap in range(1, halfway + 1):
+        from_left = lax.ppermute(from_left, axis, right)
+        out = lax.dynamic_update_slice_in_dim(
+            out, from_left, (index - lap) % length * rows, axis=dim
+        )
+        if lap < length - halfway:
+            from_right = lax.ppermute(from_right, axis, left)
+            out = lax.dynamic_update_slice_in_dim(
+                out, from_right, (index + lap) % length * rows, axis=dim
+            )
+    return out
 
 
 def norm_rows(values, gains, offset):
@@ -238,7 +259,7 @@
         ) = stored[depth]
         grad_b_down = jnp.sum(grad_hidden, 0)
         grad_branch = grad_hidden.astype(jnp.bfloat16)
-        grad_branch_rows = lax.all_gather(grad_branch, "heads", axis=0, tiled=True)
+        grad_branch_rows = ring_gather(grad_branch, "heads", 0)
         grad_activated = matmul_nt(grad_branch_rows, full_down)
         gelu_values, gelu_pull = jax.vjp(gelu_exact, pre_act)
         grad_pre = gelu_pull(grad_activated)[0].astype(jnp.bfloat16)

time: 908 us -> 914 us (level)
    all_gather x1 -> x0, waiting for transfers between devices: 28.6 us -> none  [per_device(): grad_branch_rows = lax.all_gather(grad_branch, 'heads', axis=0, tiled=True)]
    ppermute x0 -> x3, waiting for transfers between devices: none -> 25.3 us  [the longest x2 25.3 us: ring_gather(): from_left = lax.ppermute(from_left, axis, right)]
  transfers between devices with their start and end apart: 10 -> 12, of which waited for: 10 -> 11; matrix products, arithmetic and copies ran while one was open for 4% -> 4% of each run, Pallas kernels for 0% -> 0%
where the time goes in v1:
time: 914 us; the launch traced here: 910 us
  waiting for transfers between devices  560 us (61%)
  matrix products  154 us (17%)
  local copies, waits for them, and re-layouts  86.4 us (9%)
  blocking collectives  64.3 us (7%)
  other arithmetic  27.5 us (3%)
  between operations  14.8 us (2%)
    psum x1, waiting for transfers between devices, per_device(): lax.psum((stacked(0), stacked(1), stacked(2), stacked(3), stacked(4), sta...  164 us
    psum x1, waiting for transfers between devices, per_device(): lax.psum((grad_w_in, grad_b_in, grad_pos, grad_cls, stacked(7), stacked(8...  152 us
    psum x1, blocking collectives, per_device(): lax.psum((grad_w_in, grad_b_in, grad_pos, grad_cls, stacked(7), stacked(8...  41.2 us
    dot_general x10, matrix products, matmul(): return jnp.dot(matrix, other, preferred_element_type=jnp.float32)  40.7 us
    reduce_scatter x1, waiting for transfers between devices, per_device(): lax.psum_scatter(matmul_nt(grad_pre, full_up).astype(jnp.bfloat16), 'head...  37.8 us
    reduce_scatter x1, waiting for transfers between devices, per_device(): lax.psum_scatter(matmul(attended, weight_out).astype(jnp.bfloat16), 'head...  37.4 us
    reduce_scatter x1, waiting for transfers between devices, per_device(): lax.psum_scatter(matmul(activated, full_down).astype(jnp.bfloat16), 'head...  37.2 us
    all_gather x1, waiting for transfers between devices, per_device(): rows_norm = lax.all_gather(normed1, 'heads', axis=0, tiled=True)  31.1 us
  transfers between devices with their start and end apart: 12, of which 11 were waited for; matrix products, arithmetic and copies ran while one was open for 4% of the time, Pallas kernels for 0%

profile of v1, /device:TPU:0, one launch (start us, length us, event | category | flops | bytes accessed | tf_op | source)
XLA Modules:
  0.0 910.0 jit_solution(6197123498587982954)
XLA Ops:
  15.1 31.1 %all-gather.4.cloned.1.call-done = bf16[2048,768]{1,0:T(8,128)(2,1)} async-done(((bf16[512,768]{1,0:T(8,128)(2,1)}), bf16[2048,768]{1,0:T(8,128)(2,1)}) %all-gather.4.cloned.1.call-update) | async-done | bytes 3145744 | tf_op jit(solution)/shard_map/all_gather | solution.py:179
  52.1 3.9 convolution_convert_fusion.7
  61.6 3.9 convolution_convert_fusion.6
  72.2 12.9 %while.26 = (s32[]{:T(128)}, bf16[4,2,256,3,64]{2,1,0,4,3:T(2,128)(2,1)}, f32[4,2,3,256,1]{3,2,1,4,0:T(4,128)S(1)}, bf16[4,2,256,3,64]{2,4,3,1,0:T(8,128)(2,1)S(...) while((s32[]{:T(128)}, ...), condition=%wide.region_7.8_spmd, body=%wide.region_4.7_spmd.sunk | while | flops 103840256 | bytes 6358625 | solution.py:183
  91.9 37.4 %reduce-scatter.5.cloned.1.call-done = bf16[512,768]{1,0:T(8,128)(2,1)} async-done(((bf16[2048,768]{1,0:T(8,128)(2,1)}), bf16[512,768]{1,0:T(8,128)(2,1)}) %reduce-scatter.5.cloned.1.call-update) | async-done | bytes 786448 | tf_op jit(solution)/shard_map/reduce_scatter | solution.py:188
  133.3 28.4 %all-gather.6.cloned.1.call-done = bf16[2048,768]{1,0:T(8,128)(2,1)} async-done(((bf16[512,768]{1,0:T(8,128)(2,1)}), bf16[2048,768]{1,0:T(8,128)(2,1)}) %all-gather.6.cloned.1.call-update) | async-done | bytes 3145744 | tf_op jit(solution)/shard_map/all_gather | solution.py:193
  161.7 18.8 %multiply_convert_fusion.1 = (bf16[2048,768]{1,0:T(8,128)(2,1)S(1)}, f32[2048,768]{1,0:T(8,128)}, f32[2048,768]{1,0:T(8,128)}) fusion(f32[768]{0:T(1024)S(1)} %convert_reduce_fusion.6, bf16[2048,768]{1,0:T(8,128)(2,1)} %all-gather.6.cloned.1.call-done, bf16[1,768,768]{2,1,0:T(8,128)(2,1)} %param.42), kind=kOutput, calls=%fused_computation.70 | convolution fusion | flops 2519728128 | bytes 20057088 | tf_op jit(solution)/shard_map/dot_general | solution.py:44
  182.3 3.9 convolution_convert_fusion.3
  187.2 37.2 %reduce-scatter.7.cloned.1.call-done = bf16[512,768]{1,0:T(8,128)(2,1)} async-done(((bf16[2048,768]{1,0:T(8,128)(2,1)}), bf16[512,768]{1,0:T(8,128)(2,1)}) %reduce-scatter.7.cloned.1.call-update) | async-done | bytes 786448 | tf_op jit(solution)/shard_map/reduce_scatter | solution.py:199
  234.7 17.9 %collective-permute-done = bf16[512,768]{1,0:T(8,128)(2,1)} collective-permute-done((bf16[512,768]{1,0:T(8,128)(2,1)}, bf16[512,768]{1,0:T(8,128)(2,1)}, u32[]{:S(2)}, u32[]{:S(2)}) %collective-permute-start) | collective-permute-done | bytes 786464 | tf_op jit(solution)/shard_map/ppermute | solution.py:20
  256.8 7.5 collective-permute-done.2
  266.3 10.1 %convert_reduce_fusion = (f32[768]{0:T(1024)}, bf16[2048,768]{1,0:T(8,128)(2,1)S(1)}) fusion(f32[2048,768]{1,0:T(8,128)} %get-tuple-element.242, bf16[2048,768]{1,0:T(8,128)(2,1)} %constant_dynamic-update-slice_fusion, bf16[1,768,768]{2,1,0:T(8,128)(2,1)S(1)} %copy-done.57, f32[2048,768]{1,0:T(8,128)} %get-tuple-element.257, f32[768]{0:T(1024)S(1)} %convert_reduce_fusion.6), kind=kOutput, calls=%fused_computation.67 | convolution fusion | flops 2442657024 | bytes 20060160 | tf_op jit(solution)/shard_map/dot_general | solution.py:54
  278.2 4.0 convolution_convert_fusion.2
  282.3 37.8 %reduce-scatter.9.cloned.1.call-done = bf16[512,768]{1,0:T(8,128)(2,1)} async-done(((bf16[2048,768]{1,0:T(8,128)(2,1)}), bf16[512,768]{1,0:T(8,128)(2,1)}) %reduce-scatter.9.cloned.1.call-update) | async-done | bytes 786448 | tf_op jit(solution)/shard_map/reduce_scatter | solution.py:269
  328.0 28.2 %all-gather.8.cloned.1.call-done = bf16[2048,768]{1,0:T(8,128)(2,1)} async-done(((bf16[512,768]{1,0:T(8,128)(2,1)}), bf16[2048,768]{1,0:T(8,128)(2,1)}) %all-gather.8.cloned.1.call-update) | async-done | bytes 3145744 | tf_op jit(solution)/shard_map/all_gather | solution.py:279
  356.3 3.9 convolution_convert_fusion.5
  367.4 69.2 %while.27 = (s32[]{:T(128)}, bf16[4,2,256,3,64]{2,1,0,4,3:T(2,128)(2,1)}, bf16[4,2,256,3,64]{2,1,0,4,3:T(2,128)(2,1)}, bf16[4,2,256,3,64]{2,1,0,4,3:T(2,128)(2,1...) while((s32[]{:T(128)}, ...), condition=%wide.region_18.19_spmd, body=%wide.region_16.18_spmd.sunk | while | flops 257789440 | bytes 21261944 | solution.py:283
  373.9 3.5 fusion.189
  380.4 3.5 fusion.187
  391.2 3.5 fusion.189
  397.7 3.5 fusion.187
  408.5 3.5 fusion.189
  415.0 3.4 fusion.187
  425.8 3.5 fusion.189
  452.7 7.1 convolution_bitcast_fusion
  459.7 4.1 convolution_bitcast_fusion.1
  473.2 17.5 %reduce-scatter.11.cloned.1.call-done = bf16[512,768]{1,0:T(8,128)(2,1)} async-done(((bf16[2048,768]{1,0:T(8,128)(2,1)}), bf16[512,768]{1,0:T(8,128)(2,1)}) %reduce-scatter.11.cloned.1.call-update) | async-done | bytes 786448 | tf_op jit(solution)/shard_map/reduce_scatter | solution.py:303
  505.8 23.1 %psum.139 = f32[1,768]{1,0:T(1,128)} all-reduce(f32[1,768]{1,0:T(1,128)S(1)} %stack.33), channel_id=1, replica_groups=mesh['rows'=8,'heads'=4] {'rows'}, use_global_device_ids=true, to_apply=%region_48.49 | all-reduce | flops 768 | bytes 6144 | tf_op jit(solution)/shard_map/psum | solution.py:356
  529.0 41.2 %all-reduce.6 = (f32[768]{0:T(1024)}, f32[1,768]{1,0:T(1,128)}, f32[1,768]{1,0:T(1,128)}, f32[1,768]{1,0:T(1,128)}, f32[1,768]{1,0:T(1,128)}, /*index=5*/f32[1,768]{1,0:T(1,128)}, f32[96]{0:T(128)}) all-reduce(f32[768]{0:T(1024)S(1)} %get-tuple-element.235, ...), channel_id=1, replica_groups=mesh['rows'=8,'heads'=4] {'rows','heads'}, use_global_device_ids=true, to_apply=%region_27.28 | all-reduce | flops 4704 | bytes 37632 | tf_op jit(solution)/shard_map/psum | solution.py:371
  571.1 164.5 %all-reduce.14.cloned.1.call-done = (f32[1,768,192]{1,2,0:T(8,128)}, f32[1,768,192]{1,2,0:T(8,128)}, f32[1,768,192]{1,2,0:T(8,128)}, f32[1,192,768]{2,1,0:T(8,12...) async-done(((f32[1,768,192]{1,2,0:T(8,128)}, f32[1,768,192]{1,2,0:T(8,128)}, f32[1,768,192]{1,2,0:T(8,128)}, f32[1,192,768]{2,1,0:T(8,128)}, f32[1,768,768]{2,1,0:T(8,128)}, ...) | async-done | bytes 7077904 | tf_op jit(solution)/shard_map/psum | solution.py:356
  735.6 152.2 %all-reduce.12.cloned.1.call-done = (f32[48,768]{1,0:T(8,128)}, f32[256,768]{1,0:T(8,128)}, f32[1000,768]{1,0:T(8,128)}, f32[768,96]{0,1:T(8,128)}) async-done(((f32[48,768]{1,0:T(8,128)}, f32[256,768]{1,0:T(8,128)}, f32[1000,768]{1,0:T(8,128)}, f32[768,96]{0,1:T(8,128)}), (f32[48,768]{1,0:T(8,128)}, f32[256,768]{1,0:T(8,128)}, f32[1000,768]{1,0:T(8,128)}, ...) | async-done | bytes 4300816 | tf_op jit(solution)/shard_map/psum | solution.py:371
  891.5 3.8 copy.167
  (339 shorter events, 183.0 us)
Async XLA Ops:
  7.2 4.8 copy-start
  7.2 39.1 %all-gather.4.cloned.1.call-start = ((), (), s32[]{:S(2)}) async-start(), calls=%async_computation.4 | async-start | bytes 3932160 | tf_op jit(solution)/shard_map/all_gather | solution.py:179
  13.3 33.0 %copy-start.39 = (bf16[1,768,192]{1,2,0:T(8,128)(2,1)S(1)}, bf16[1,768,192]{1,2,0:T(8,128)(2,1)}, u32[]{:S(2)}) copy-start(bf16[1,768,192]{1,2,0:T(8,128)(2,1)} %param.38) | copy-start | bytes 884740
  14.9 114.4 %reduce-scatter.5.cloned.1.call-start = ((), (), s32[]{:S(2)}) async-start(), calls=%async_computation.5 | async-start | bytes 3932160 | tf_op jit(solution)/shard_map/reduce_scatter | solution.py:188
  56.1 5.5 copy-start.31
  72.2 16.2 %copy-start.37 = (bf16[1,192,768]{2,1,0:T(8,128)(2,1)S(1)}, bf16[1,192,768]{2,1,0:T(8,128)(2,1)}, u32[]{:S(2)}) copy-start(bf16[1,192,768]{2,1,0:T(8,128)(2,1)} %param.39) | copy-start | bytes 884740
  91.2 70.6 %all-gather.6.cloned.1.call-start = ((), (), s32[]{:S(2)}) async-start(), calls=%async_computation.6 | async-start | bytes 3932160 | tf_op jit(solution)/shard_map/all_gather | solution.py:193
  133.1 91.3 %reduce-scatter.7.cloned.1.call-start = ((), (), s32[]{:S(2)}) async-start(), calls=%async_computation.7 | async-start | bytes 3932160 | tf_op jit(solution)/shard_map/reduce_scatter | solution.py:199
  161.7 20.5 %copy-start.56 = (bf16[1,768,768]{2,1,0:T(8,128)(2,1)S(1)}, bf16[1,768,768]{2,1,0:T(8,128)(2,1)}, u32[]{:S(2)}) copy-start(bf16[1,768,768]{2,1,0:T(8,128)(2,1)} %param.44) | copy-start | bytes 3538948
  186.2 40.8 %copy-start.24 = (bf16[768,96]{0,1:T(8,128)(2,1)S(1)}, bf16[768,96]{0,1:T(8,128)(2,1)}, u32[]{:S(2)}) copy-start(bf16[768,96]{0,1:T(8,128)(2,1)} %param.46) | copy-start | bytes 442372
  186.2 41.1 %copy-start.54 = (f32[96]{0:T(128)S(1)}, f32[96]{0:T(128)}, u32[]{:S(2)}) copy-start(f32[96]{0:T(128)} %param.47) | copy-start | bytes 1156
  186.2 133.9 %reduce-scatter.9.cloned.1.call-start = ((), (), s32[]{:S(2)}) async-start(), calls=%async_computation.8 | async-start | bytes 3932160 | tf_op jit(solution)/shard_map/reduce_scatter | solution.py:269
  187.2 40.4 %copy-start.23 = (f32[512,48]{0,1:T(8,128)S(1)}, f32[512,48]{0,1:T(8,128)}, u32[]{:S(2)}) copy-start(f32[512,48]{0,1:T(8,128)} %param.27) | copy-start | bytes 294916
  187.2 40.5 %copy-start.29 = (f32[512,48]{0,1:T(8,128)S(1)}, f32[512,48]{0,1:T(8,128)}, u32[]{:S(2)}) copy-start(f32[512,48]{0,1:T(8,128)} %param.48) | copy-start | bytes 294916
  232.9 19.6 %collective-permute-start = (bf16[512,768]{1,0:T(8,128)(2,1)}, bf16[512,768]{1,0:T(8,128)(2,1)}, u32[]{:S(2)}, u32[]{:S(2)}) collective-permute-start(bf16[512,768]{1,0:T(8,128)(2,1)} %get-tuple-element.240), channel_id=1, source_target_pairs={{0,1},{1,2},{2,3},{3,0},{4,5},{5,6},{6,7},{7,4},{8,9},{9,10},{10,1... | collective-permute-start | bytes 2359304 | tf_op jit(solution)/shard_map/ppermute | solution.py:20
  232.9 21.8 %collective-permute-start.1 = (bf16[512,768]{1,0:T(8,128)(2,1)}, bf16[512,768]{1,0:T(8,128)(2,1)}, u32[]{:S(2)}, u32[]{:S(2)}) collective-permute-start(bf16[512,768]{1,0:T(8,128)(2,1)} %get-tuple-element.240), channel_id=1, source_target_pairs={{0,3},{1,0},{2,1},{3,2},{4,7},{5,4},{6,5},{7,6},{8,11},{9,8},{10,9... | collective-permute-start | bytes 2359304 | tf_op jit(solution)/shard_map/ppermute | solution.py:25
  252.5 11.7 %collective-permute-start.2 = (bf16[512,768]{1,0:T(8,128)(2,1)}, bf16[512,768]{1,0:T(8,128)(2,1)}, u32[]{:S(2)}, u32[]{:S(2)}) collective-permute-start(bf16[512,768]{1,0:T(8,128)(2,1)} %collective-permute-done), channel_id=1, source_target_pairs={{0,1},{1,2},{2,3},{3,0},{4,5},{5,6},{6,7},{7,4},{8,9},{9,10},{10,1... | collective-permute-start | bytes 2359304 | tf_op jit(solution)/shard_map/ppermute | solution.py:20
  252.5 13.8 %copy-start.57 = (bf16[1,768,768]{2,1,0:T(8,128)(2,1)S(1)}, bf16[1,768,768]{2,1,0:T(8,128)(2,1)}, u32[]{:S(2)}) copy-start(bf16[1,768,768]{2,1,0:T(8,128)(2,1)} %param.44) | copy-start | bytes 3538948
  266.3 11.8 %copy-start.58 = (bf16[1,768,768]{2,1,0:T(8,128)(2,1)S(1)}, bf16[1,768,768]{2,1,0:T(8,128)(2,1)}, u32[]{:S(2)}) copy-start(bf16[1,768,768]{2,1,0:T(8,128)(2,1)} %param.42) | copy-start | bytes 3538948
  282.2 74.1 %all-gather.8.cloned.1.call-start = ((), (), s32[]{:S(2)}) async-start(), calls=%async_computation.9 | async-start | bytes 3932160 | tf_op jit(solution)/shard_map/all_gather | solution.py:279
  326.5 29.8 %copy-start.38 = (bf16[1,192,768]{2,1,0:T(8,128)(2,1)S(1)}, bf16[1,192,768]{2,1,0:T(8,128)(2,1)}, u32[]{:S(2)}) copy-start(bf16[1,192,768]{2,1,0:T(8,128)(2,1)} %param.39) | copy-start | bytes 884740
  327.6 163.1 %reduce-scatter.11.cloned.1.call-start = ((), (), s32[]{:S(2)}) async-start(), calls=%async_computation.10 | async-start | bytes 3932160 | tf_op jit(solution)/shard_map/reduce_scatter | solution.py:303
  436.6 9.6 %copy-start.32 = (bf16[1,768,192]{1,2,0:T(8,128)(2,1)S(1)}, bf16[1,768,192]{1,2,0:T(8,128)(2,1)}, u32[]{:S(2)}) copy-start(bf16[1,768,192]{1,2,0:T(8,128)(2,1)} %param.37) | copy-start | bytes 884740
  452.6 283.1 %all-reduce.14.cloned.1.call-start = ((), (), s32[]{:S(2)}) async-start(), calls=%async_computation.12 | async-start | bytes 14155776 | tf_op jit(solution)/shard_map/psum | solution.py:356
  452.6 7.1 copy-start.55
  452.6 7.1 copy-start.62
  471.1 416.8 %all-reduce.12.cloned.1.call-start = ((), (), s32[]{:S(2)}) async-start(), calls=%async_computation.11 | async-start | bytes 8601600 | tf_op jit(solution)/shard_map/psum | solution.py:371
  503.8 25.2 %copy-start.42 = (f32[768]{0:T(1024)S(1)}, f32[768]{0:T(1024)}, u32[]{:S(2)}) copy-start(f32[768]{0:T(1024)} %get-tuple-element.173) | copy-start | bytes 9220
  503.8 25.2 %copy-start.41 = (f32[768]{0:T(1024)S(1)}, f32[768]{0:T(1024)}, u32[]{:S(2)}) copy-start(f32[768]{0:T(1024)} %get-tuple-element.177) | copy-start | bytes 9220
  503.8 66.4 %copy-start.30 = (f32[512,48]{0,1:T(8,128)S(1)}, f32[512,48]{0,1:T(8,128)}, u32[]{:S(2)}) copy-start(f32[512,48]{0,1:T(8,128)} %param.48) | copy-start | bytes 294916
  503.8 66.4 %copy-start.36 = (bf16[48,768]{1,0:T(8,128)(2,1)S(1)}, bf16[48,768]{1,0:T(8,128)(2,1)}, u32[]{:S(2)}) copy-start(bf16[48,768]{1,0:T(8,128)(2,1)} %param.30) | copy-start | bytes 221188
  891.5 5.5 copy-start.26
  (43 other events, 93.0 us)
Sparse Core Ops, SparseCore 0:
  15.0 31.2 all-gather.3
  91.3 37.9 reduce-scatter.4
  133.2 28.5 all-gather.5
  186.3 37.9 reduce-scatter.6
  282.3 37.7 reduce-scatter.8
  327.7 28.5 all-gather.7
  452.7 37.9 reduce-scatter.10
  496.9 238.6 all-reduce.13
  744.6 143.1 all-reduce.11
